TPU v7x, 512 devices: a whole 4x8x8 slice. The times are simulated.
512 devices in a mesh: band: 32 (over x, y_lo, core), grid: 16 (over z, y_hi).
Axes of the slice: x: 4, y: 8 (y_hi: 2, y_lo: 4; y = y_hi * 4 + y_lo), z: 8, core: 2. Of those that a mesh axis runs over, the one named last changes fastest.
Arguments:
- orbitals: bfloat16 [64, 160, 25600], P('band', 'grid'), may hold values from -6 to 6
- source_index: int32 [2], replicated, may hold values from 0 to 63
Outputs:
- fock_exchange: bfloat16 [64, 160, 25600], P('band', 'grid')
All inputs are finite; a program needn't handle non-finite values.
Results may differ from a plain program's by a relative error of at most 0.012.
The roundings to bfloat16 on the way count: a program that leaves them out, or rounds other values in their place, can miss the bound.
Values may be sent and summed in bfloat16 or wider, within the bound.
A program may use at most 64 MiB of HBM per device.

v0:
```python
import math
import jax
import jax.numpy as jnp
from jax import lax
from jax.sharding import PartitionSpec as P

spacing = 0.3


def broadcast(x, axis, root):
    mine = lax.axis_index(axis) == root
    return lax.psum(jnp.where(mine, x, jnp.zeros_like(x)), axis)


def cas_table(extent):
    wavenum = jnp.arange(extent, dtype=jnp.int32)
    products_mod = wavenum[:, None] * wavenum[None, :] % extent
    radians = products_mod.astype(jnp.float32) * (2.0 * math.pi / extent)
    return ((jnp.cos(radians) + jnp.sin(radians)) / math.sqrt(extent)).astype(jnp.bfloat16)


def wave_square(indices, extent):
    folded = jnp.minimum(indices, extent - indices).astype(jnp.float32)
    return folded * folded


def transform(grid_data, cas_matrix, pattern):
    return jnp.einsum(pattern, grid_data, cas_matrix, preferred_element_type=jnp.float32)


def potentials(pair_rho, cas_matrix, kernel_block):
    along_z = transform(pair_rho, cas_matrix, "pxyz,kz->pxyk").astype(jnp.bfloat16)
    along_y = transform(along_z, cas_matrix, "pxyz,ky->pxkz").astype(jnp.bfloat16)
    scaled = (
        kernel_block
        * transform(
            lax.all_to_all(along_y, "grid", split_axis=2, concat_axis=1, tiled=True),
            cas_matrix,
            "pxyz,kx->pkyz",
        )
    ).astype(jnp.bfloat16)
    back_x = transform(scaled, cas_matrix, "pxyz,kx->pkyz").astype(jnp.bfloat16)
    returned = lax.all_to_all(back_x, "grid", split_axis=1, concat_axis=2, tiled=True)
    again_y = transform(returned, cas_matrix, "pxyz,ky->pxkz").astype(jnp.bfloat16)
    return transform(again_y, cas_matrix, "pxyz,kz->pxyk")


def fetch_source(orbitals, which):
    local_count = orbitals.shape[0]
    local_slab = lax.dynamic_index_in_dim(orbitals, which % local_count, 0, keepdims=False)
    return broadcast(local_slab, "band", which // local_count)


def shards(orbitals, source_index):
    local_count = orbitals.shape[0]
    planes = orbitals.shape[1]
    extent = planes * lax.axis_size("grid")
    orbitals = orbitals.reshape(local_count, planes, extent, extent)
    source_count = source_index.shape[0]
    cas_matrix = cas_table(extent)
    columns = extent // lax.axis_size("grid")
    offset = lax.axis_index("grid") * columns
    square_x = wave_square(jnp.arange(extent, dtype=jnp.int32), extent)
    square_y = wave_square(offset + jnp.arange(columns, dtype=jnp.int32), extent)
    total_sq = square_x[:, None, None] + square_y[None, :, None] + square_x[None, None, :]
    strength = (extent * spacing) ** 2 / math.pi
    kernel_block = jnp.where(total_sq > 0, strength / (total_sq + 1.0), 0.0)
    fetched = None
    fetched = [fetch_source(orbitals, source_index[number]) for number in range(source_count)]
    stacked = jnp.stack(fetched)[:, None].astype(jnp.float32)
    pair_rho = (stacked * orbitals[None].astype(jnp.float32)).astype(jnp.bfloat16)
    pair_rho = pair_rho.reshape(source_count * local_count, planes, extent, extent)
    potential = potentials(pair_rho, cas_matrix, kernel_block)
    potential = potential.reshape(source_count, local_count, planes, extent, extent)
    summed_total = jnp.sum(stacked * potential, axis=0)
    result = (-summed_total).astype(jnp.bfloat16)
    return result.reshape(local_count, planes, extent * extent)


def solution(mesh):
    return jax.shard_map(
        shards,
        mesh=mesh,
        in_specs=(P("band", "grid", None), P()),
        out_specs=P("band", "grid", None),
        check_vma=False,
    )
```

profile of v0, /device:TPU:54, one launch (start us, length us, event | category | flops | bytes accessed | tf_op | source)
XLA Modules:
  0.0 598.6 jit_solution(17245803974825692510)
XLA Ops:
  6.5 0.0 all-reduce.3.cloned.1.call-start
  6.5 1.3 fusion.89
  13.0 3.7 reshape.107
  16.7 1.3 dynamic-slice_select_fusion.1
  18.0 0.0 all-reduce.3.cloned.1.call-update
  18.0 281.7 %all-reduce.3.cloned.1.call-done = (bf16[1,10,160,160]{3,2,0,1:T(8,128)(2,1)}, bf16[1,10,160,160]{3,2,0,1:T(8,128)(2,1)}) async-done(((bf16[1,10,160,160]{3,2,0,1:T(8,128)(2,1)}, bf16[1,10,160,160]{3,2,0,1:T(8,128)(2,1)}), (bf16[1,10,160,160]{3,2,0,1:T(8,128)(2,1)}, bf16[1,10,160,160]{3,2,0,1:T(8,128)(2,1)})) %all-reduce.3.cloned.1.call-update) | async-done | bytes 1024016 | tf_op jit(solution)/shard_map/psum | solution.py:12
  299.7 5.3 multiply_convert_fusion.1
  305.0 4.6 convert_bitcast_fusion.1
  309.6 4.2 copy.35
  313.8 12.8 %all-to-all-start = ((bf16[4,10,160,160]{3,0,1,2:T(4,128)(2,1)}), bf16[4,10,160,160]{3,0,1,2:T(4,128)(2,1)S(1)}, u32[]{:S(2)}, u32[]{:S(2)}) async-start(bf16[4,10,160,160]{3,0,1,2:T(4,128)(2,1)} %copy.35), calls=%async_computation | async-start | bytes 6553600 | tf_op jit(solution)/shard_map/all_to_all | solution.py:37
  326.6 0.1 broadcast_add_fusion
  326.7 1.6 fusion.30
  328.2 145.4 %all-to-all-done = bf16[4,10,160,160]{3,0,1,2:T(4,128)(2,1)S(1)} async-done(((bf16[4,10,160,160]{3,0,1,2:T(4,128)(2,1)}), bf16[4,10,160,160]{3,0,1,2:T(4,128)(2,1)S(1)}, u32[]{:S(2)}, u32[]{:S(2)}) %all-to-all-start) | async-done | bytes 2048032 | tf_op jit(solution)/shard_map/all_to_all | solution.py:37
  473.7 2.8 copy.37
  476.5 5.9 convert_bitcast_fusion
  482.3 2.5 copy.39
  484.9 90.1 %all_to_all.36 = bf16[4,160,10,160]{3,0,2,1:T(4,128)(2,1)S(1)} all-to-all(bf16[4,160,10,160]{3,0,2,1:T(4,128)(2,1)S(1)} %copy.39), channel_id=1, replica_groups=mesh['band'=32,'grid'=16] {'grid'}, dimensions={1} | all-to-all | bytes 4096000 | tf_op jit(solution)/shard_map/all_to_all | solution.py:43
  574.9 1.3 copy.40
  576.3 5.3 fusion.3
  581.5 5.0 multiply_reduce_fusion
  586.6 0.4 negate_convert_fusion
  587.0 2.7 reshape.112
  589.7 2.0 copy.45
  (2 shorter events, 0.0 us)
Async XLA Ops:
  6.5 293.2 %all-reduce.3.cloned.1.call-start = ((), (), s32[]{:S(2)}) async-start(), calls=%async_computation.2 | async-start | bytes 3276800 | tf_op jit(solution)/shard_map/psum | solution.py:12
  313.8 159.9 %all-to-all-start = ((bf16[4,10,160,160]{3,0,1,2:T(4,128)(2,1)}), bf16[4,10,160,160]{3,0,1,2:T(4,128)(2,1)S(1)}, u32[]{:S(2)}, u32[]{:S(2)}) async-start(bf16[4,10,160,160]{3,0,1,2:T(4,128)(2,1)} %copy.35), calls=%async_computation | async-start | bytes 6553600 | tf_op jit(solution)/shard_map/all_to_all | solution.py:37
Sparse Core Ops, SparseCore 0:
  18.1 281.5 all-reduce.2
where the time goes:
time: 599 us
  waiting for transfers between devices  427 us (71%)
  blocking collectives  90.1 us (15%)
  local copies, waits for them, and re-layouts  20.6 us (3%)
  between operations  18.5 us (3%)
  matrix products  15.7 us (3%)
  other arithmetic  13.7 us (2%)
  starting transfers between devices  12.8 us (2%)
    psum x1, waiting for transfers between devices, broadcast(): return lax.psum(jnp.where(mine, x, jnp.zeros_like(x)), axis)  282 us
    all_to_all x1, waiting for transfers between devices, potentials(): lax.all_to_all(along_y, 'grid', split_axis=2, concat_axis=1, tiled=True)  145 us
    all_to_all x1, blocking collectives, potentials(): lax.all_to_all(back_x, 'grid', split_axis=1, concat_axis=2, tiled=True)  90.1 us
    dot_general x3, matrix products, transform(): jnp.einsum(pattern, grid_data, cas_matrix, preferred_element_type=jnp.flo...  15.7 us
    all_to_all x1, starting transfers between devices, potentials(): lax.all_to_all(along_y, 'grid', split_axis=2, concat_axis=1, tiled=True)  12.8 us
  transfers between devices with their start and end apart: 2, of which 2 were waited for; matrix products, arithmetic and copies ran while one was open for 0% of the time, Pallas kernels for 0%

commit v1 on v0

--- a/solution.py
+++ b/solution.py
@@ -9,7 +9,7 @@
 
 def broadcast(x, axis, root):
     mine = lax.axis_index(axis) == root
-    return lax.psum(jnp.where(mine, x, jnp.zeros_like(x)), axis)
+    return jnp.sum(lax.all_gather(jnp.where(mine, x, jnp.zeros_like(x)), axis), axis=0)
 
 
 def cas_table(extent):

time: 599 us -> 671 us (1.12)
  the two profiles are of different devices: /device:TPU:54 before, /device:TPU:50 now
where the time goes in v1:
time: 671 us; the launch traced here: 670 us
  waiting for transfers between devices  409 us (61%)
  blocking collectives  135 us (20%)
  other arithmetic  45.6 us (7%)
  local copies, waits for them, and re-layouts  28.3 us (4%)
  matrix products  21 us (3%)
  between operations  18.6 us (3%)
  starting transfers between devices  12.8 us (2%)
    all_gather x2, waiting for transfers between devices, broadcast(): lax.all_gather(jnp.where(mine, x, jnp.zeros_like(x)), axis)  290 us
    all_to_all x1, blocking collectives, potentials(): lax.all_to_all(back_x, 'grid', split_axis=1, concat_axis=2, tiled=True)  135 us
    all_to_all x1, waiting for transfers between devices, potentials(): lax.all_to_all(along_y, 'grid', split_axis=2, concat_axis=1, tiled=True)  118 us
    reduce_sum x2, other arithmetic, broadcast(): jnp.sum(lax.all_gather(jnp.where(mine, x, jnp.zeros_like(x)), axis), axis=0)  32 us
    dot_general x3, matrix products, transform(): jnp.einsum(pattern, grid_data, cas_matrix, preferred_element_type=jnp.flo...  21 us
  transfers between devices with their start and end apart: 3, of which 3 were waited for; matrix products, arithmetic and copies ran while one was open for 3% of the time, Pallas kernels for 0%

profile of v1, /device:TPU:50, one launch (start us, length us, event | category | flops | bytes accessed | tf_op | source)
XLA Modules:
  0.0 670.5 jit_solution(2784069435522040971)
XLA Ops:
  6.5 0.0 all-gather.3.cloned.1.call-start
  6.5 1.3 fusion.89
  13.0 3.7 reshape.101
  16.7 0.0 copy-start
  16.7 1.4 dynamic-slice_select_fusion.1
  18.1 0.0 all-gather.3.cloned.1.call-update
  18.2 0.0 all-gather.5.cloned.1.call-start
  18.2 0.7 all-gather.5.cloned.1.call-update
  18.9 153.4 %all-gather.3.cloned.1.call-done = bf16[32,10,160,160]{3,2,0,1:T(8,128)(2,1)} async-done(((bf16[1,10,160,160]{3,2,0,1:T(8,128)(2,1)}), bf16[32,10,160,160]{3,2,0,1:T(8,128)(2,1)}) %all-gather.3.cloned.1.call-update) | async-done | bytes 16384016 | tf_op jit(solution)/shard_map/all_gather | solution.py:12
  172.3 16.0 %reduce_sum.33 = bf16[10,160,160]{2,1,0:T(8,128)(2,1)} reduce(bf16[32,10,160,160]{3,2,0,1:T(8,128)(2,1)} %all-gather.3.cloned.1.call-done, bf16[]{:T(256)} %constant.72.clone.1), dimensions={0}, to_apply=%region_0.1 | reduce | flops 7936000 | bytes 16896002 | tf_op jit(solution)/shard_map/reduce_sum | solution.py:12
  188.3 0.0 copy-done
  188.3 137.0 %all-gather.5.cloned.1.call-done = bf16[32,10,160,160]{3,2,0,1:T(8,128)(2,1)} async-done(((bf16[1,10,160,160]{3,2,0,1:T(8,128)(2,1)}), bf16[32,10,160,160]{3,2,0,1:T(8,128)(2,1)}) %all-gather.5.cloned.1.call-update) | async-done | bytes 16384016 | tf_op jit(solution)/shard_map/all_gather | solution.py:12
  325.3 16.0 %reduce_sum.34 = bf16[10,160,160]{2,1,0:T(8,128)(2,1)} reduce(bf16[32,10,160,160]{3,2,0,1:T(8,128)(2,1)} %all-gather.5.cloned.1.call-done, bf16[]{:T(256)} %constant.72.clone.1), dimensions={0}, to_apply=%region_1.2 | reduce | flops 7936000 | bytes 16896002 | tf_op jit(solution)/shard_map/reduce_sum | solution.py:12
  341.3 0.0 copy-start.1
  341.3 1.9 maximum_convert_fusion
  343.2 0.0 copy-done.1
  343.2 3.8 multiply_convert_fusion.1
  347.0 6.3 convert_bitcast_fusion.1
  353.3 6.2 copy.30
  359.5 12.8 %all-to-all-start = ((bf16[4,10,160,160]{3,0,1,2:T(4,128)(2,1)}), bf16[4,10,160,160]{3,0,1,2:T(4,128)(2,1)}, u32[]{:S(2)}, u32[]{:S(2)}) async-start(bf16[4,10,160,160]{3,0,1,2:T(4,128)(2,1)} %copy.30), calls=%async_computation | async-start | bytes 6553600 | tf_op jit(solution)/shard_map/all_to_all | solution.py:37
  372.3 0.1 broadcast_add_fusion
  372.4 1.6 fusion.30
  373.9 118.3 %all-to-all-done = bf16[4,10,160,160]{3,0,1,2:T(4,128)(2,1)} async-done(((bf16[4,10,160,160]{3,0,1,2:T(4,128)(2,1)}), bf16[4,10,160,160]{3,0,1,2:T(4,128)(2,1)}, u32[]{:S(2)}, u32[]{:S(2)}) %all-to-all-start) | async-done | bytes 2048032 | tf_op jit(solution)/shard_map/all_to_all | solution.py:37
  492.2 4.8 copy.32
  497.0 7.5 %convert_bitcast_fusion = bf16[4,160,10,160]{3,1,2,0:T(8,128)(2,1)} fusion(f32[160,10,160]{2,0,1:T(8,128)} %fusion.30, bf16[4,160,10,160]{3,0,2,1:T(4,128)(2,1)} %bitcast.45), kind=kOutput, calls=%fused_computation.13 | convolution fusion | flops 659046400 | bytes 5120000 | tf_op jit(solution)/shard_map/pxyz,kx->pkyz/dot_general | solution.py:28
  504.5 4.5 copy.34
  509.0 134.7 %all_to_all.36 = bf16[4,160,10,160]{3,0,2,1:T(4,128)(2,1)S(1)} all-to-all(bf16[4,160,10,160]{3,0,2,1:T(4,128)(2,1)S(1)} %copy.34), channel_id=1, replica_groups=mesh['band'=32,'grid'=16] {'grid'}, dimensions={1} | all-to-all | bytes 4096000 | tf_op jit(solution)/shard_map/all_to_all | solution.py:43
  643.7 3.1 copy.35
  646.9 7.2 %fusion.3 = f32[4,10,160,160]{3,2,1,0:T(8,128)} fusion(bf16[4,10,160,160]{3,0,2,1:T(4,128)(2,1)} %bitcast.43), kind=kOutput, calls=%fused_computation.5 | convolution fusion | flops 656998400 | bytes 6144000 | tf_op jit(solution)/shard_map/pxyz,kz->pxyk/dot_general | solution.py:28
  654.1 4.4 multiply_reduce_fusion
  658.5 0.4 negate_convert_fusion
  658.9 2.7 reshape.104
  661.6 2.0 copy.40
  (2 shorter events, 0.0 us)
Async XLA Ops:
  6.5 165.8 %all-gather.3.cloned.1.call-start = ((), (), s32[]{:S(2)}) async-start(), calls=%async_computation.2 | async-start | bytes 27033600 | tf_op jit(solution)/shard_map/all_gather | solution.py:12
  16.7 171.7 %copy-start = (bf16[2,10,160,160]{3,2,0,1:T(8,128)(2,1)}, bf16[2,10,160,160]{3,2,0,1:T(8,128)(2,1)S(1)}, u32[]{:S(2)}) copy-start(bf16[2,10,160,160]{3,2,0,1:T(8,128)(2,1)S(1)} %reshape.101) | copy-start | bytes 3072004
  18.2 307.1 %all-gather.5.cloned.1.call-start = ((), (), s32[]{:S(2)}) async-start(), calls=%async_computation.3 | async-start | bytes 27033600 | tf_op jit(solution)/shard_map/all_gather | solution.py:12
  341.3 1.9 copy-start.1
  359.5 132.7 %all-to-all-start = ((bf16[4,10,160,160]{3,0,1,2:T(4,128)(2,1)}), bf16[4,10,160,160]{3,0,1,2:T(4,128)(2,1)}, u32[]{:S(2)}, u32[]{:S(2)}) async-start(bf16[4,10,160,160]{3,0,1,2:T(4,128)(2,1)} %copy.30), calls=%async_computation | async-start | bytes 6553600 | tf_op jit(solution)/shard_map/all_to_all | solution.py:37
Sparse Core Ops, SparseCore 0:
  18.3 154.0 all-gather.2
  174.4 150.8 all-gather.4
